TPU v7x, 32 devices: a whole 2x2x4 slice. The times are simulated.
32 devices in a mesh: lat: 8 (over y, x, core), chan: 4 (over z).
Axes of the slice: x: 2, y: 2, z: 4, core: 2. Of those that a mesh axis runs over, the one named last changes fastest.
Arguments:
- state: bfloat16 [256, 64, 1440], P('chan', 'lat'), may hold values from -6 to 6
- kernel: bfloat16 [3, 3, 256, 256], replicated, may hold values from -0.125 to 0.125
- bias: float32 [256], P('chan'), may hold values from -3 to 3
- innovations: float32 [256, 8, 8, 1024], P('chan', 'lat'), may hold values from -6 to 6
- interp: bfloat16 [4, 8, 8, 1024], P(None, 'lat'), may hold values from 0 to 1
- cells: int32 [8, 8, 1024], P('lat'), may hold values from 0 to 90719, as said below
- counts: int32 [8, 8], P('lat'), may hold values from 1 to 1024, as said below
Outputs:
- grad_state: bfloat16 [256, 64, 1440], P('chan', 'lat')
- departures: float32 [256, 8, 8, 1024], P('chan', 'lat')
Inputs may be any that keep to these rules, and one draw needn't show every extreme that they name: `cells`: every observation of slab d has its first corner in rows 8 d to 8 d + 6. `counts`: in every draw some slab receives 1024 used slots from every instrument shard.
All inputs are finite; a program needn't handle non-finite values.
Results may differ from a plain program's by a relative error of at most 0.023.
Values may be sent and summed in bfloat16 or wider, within the bound.
No kernel may reach another device: no remote copies, remote signals or barrier semaphores. Data moves between devices by JAX's collectives and lax.ppermute only.
A program may use at most 256 MiB of HBM per device.

v0:
```python
import jax
import jax.numpy as jnp
from jax import lax
from jax.sharding import PartitionSpec as P

KERNEL_SPACING = 8


def extended(block, sides, width):
    for axis, dim in sides:
        count = lax.axis_size(axis)
        forward = [(i, i + 1) for i in range(count - 1)]
        backward = [(target, source) for source, target in forward]
        low = lax.ppermute(
            lax.slice_in_dim(block, block.shape[dim] - width, None, axis=dim), axis, forward
        )
        high = lax.ppermute(lax.slice_in_dim(block, 0, width, axis=dim), axis, backward)
        block = jnp.concatenate([low, block, high], axis=dim)
    return block


def gelu_value(value):
    return 0.5 * value * (1.0 + jax.scipy.special.erf(value * 0.7071067811865476))


def gelu_slope(value):
    return (
        0.5 * (1.0 + jax.scipy.special.erf(value * 0.7071067811865476))
        + value * jnp.exp(-0.5 * value * value) * 0.3989422804014327
    )


def tap_stack(padded_field, direction_sign, row_count):
    field_pieces = []
    for row_offset in range(3):
        for column_offset in range(3):
            start_offset = KERNEL_SPACING + direction_sign * (row_offset - 1) * KERNEL_SPACING
            part = lax.slice_in_dim(padded_field, start_offset, start_offset + row_count, axis=1)
            field_pieces.append(
                jnp.roll(part, -direction_sign * (column_offset - 1) * KERNEL_SPACING, axis=2)
            )
    stacked = jnp.stack(field_pieces)
    return stacked.reshape(9 * padded_field.shape[0], row_count * padded_field.shape[2])


def channel_mix(grid_field, kernel_t, direction_sign):
    group, row_count, width = grid_field.shape
    total_channels = kernel_t.shape[0]
    owner = lax.axis_index("chan")
    padded_field = extended(grid_field, (("lat", 1),), KERNEL_SPACING)
    stacked = tap_stack(padded_field, direction_sign, row_count)
    local_weights = lax.dynamic_slice_in_dim(kernel_t, owner * group, group, 3).reshape(
        total_channels, 9 * group
    )
    return lax.psum_scatter(
        jnp.dot(local_weights, stacked, preferred_element_type=jnp.float32)
        .reshape(group * lax.axis_size("chan"), row_count, width)
        .astype(jnp.bfloat16),
        "chan",
        scatter_dimension=0,
        tiled=True,
    ).astype(jnp.float32)


def shards(state, kernel, bias, innovations, interp, cells, counts):
    group, row_count, width = state.shape
    forward_kernel = jnp.transpose(kernel, (2, 0, 1, 3))
    backward_kernel = jnp.transpose(kernel, (3, 0, 1, 2))
    pre = channel_mix(state, forward_kernel, 1) + bias[:, None, None]
    hidden = gelu_value(pre)
    flat_hidden = hidden.reshape(group, row_count * width)
    slots = jnp.arange(innovations.shape[3], dtype=jnp.int32)
    mask = (slots[None, :] < counts[0][:, None]).astype(jnp.float32)
    masked_values = innovations * mask[None, None]
    masked_weights = interp.astype(jnp.float32) * mask[None, None]
    got_values, got_weights = (
        lax.all_to_all(
            masked_values.astype(jnp.bfloat16), "lat", split_axis=2, concat_axis=1, tiled=True
        ).astype(masked_values.dtype),
        lax.all_to_all(
            masked_weights.astype(jnp.bfloat16), "lat", split_axis=2, concat_axis=1, tiled=True
        ).astype(masked_weights.dtype),
    )
    got_cells = lax.all_to_all(cells, "lat", split_axis=1, concat_axis=0, tiled=True)
    local_cells = got_cells - lax.axis_index("lat") * row_count * width
    row_index = local_cells // width
    col_index = local_cells % width
    corner_one = row_index * width + (col_index + 1) % width
    corners = [local_cells, corner_one, local_cells + width, corner_one + width]
    model = jnp.zeros(got_values.shape, jnp.float32)
    for which in range(4):
        model = model + got_weights[which][None] * jnp.take(flat_hidden, corners[which], axis=1)
    local_departures = model - got_values
    departures = lax.all_to_all(
        local_departures.astype(jnp.bfloat16), "lat", split_axis=1, concat_axis=2, tiled=True
    ).astype(local_departures.dtype)
    grad_hidden = jnp.zeros((group, row_count * width), jnp.float32)
    for which in range(4):
        grad_hidden = grad_hidden.at[:, corners[which].reshape(-1)].add(
            (got_weights[which][None] * local_departures).reshape(group, -1)
        )
    grad_pre = (grad_hidden.reshape(pre.shape) * gelu_slope(pre)).astype(jnp.bfloat16)
    grad_state = channel_mix(grad_pre, backward_kernel, -1).astype(jnp.bfloat16)
    return (grad_state, departures)


def solution(mesh):
    return jax.shard_map(
        shards,
        mesh=mesh,
        in_specs=(
            P("chan", "lat", None),
            P(),
            P("chan"),
            P("chan", "lat", None, None),
            P(None, "lat", None, None),
            P("lat", None, None),
            P("lat", None),
        ),
        out_specs=(P("chan", "lat", None), P("chan", "lat", None, None)),
        check_vma=False,
    )
```

profile of v0, /device:TPU:0, one launch (start us, length us, event | category | flops | bytes accessed | tf_op | source)
XLA Modules:
  0.0 894.1 jit_solution(1340920264573949839)
XLA Ops:
  7.2 3.6 collective-permute-start
  15.5 2.9 fusion.58
  19.5 1.8 fusion.26
  21.4 2.7 bitcast_dynamic-update-slice_fusion.5
  25.3 1.9 fusion.28
  29.9 2.9 fusion.54
  34.0 1.9 fusion.30
  35.8 2.7 bitcast_dynamic-update-slice_fusion.3
  39.9 27.0 %reshape.416 = bf16[576,11520]{1,0:T(8,128)(2,1)} reshape(bf16[9,64,8,1440]{3,2,1,0:T(8,128)(2,1)} %fusion.31) | data formatting | bytes 26542080 | tf_op jit(solution)/shard_map/reshape | solution.py:43
  66.9 28.0 %dot_general.15 = bf16[8,1440,576]{1,0,2:T(8,128)(2,1)} reshape(bf16[11520,576]{0,1:T(8,128)(2,1)} %bitcast.220) | data formatting | bytes 26542080 | tf_op jit(solution)/shard_map/dot_general | solution.py:56
  94.8 24.5 %fusion.4 = bf16[256,8,1440]{2,0,1:T(8,128)(2,1)} fusion(bf16[256,576,1]{0,1,2:T(8,128)(2,1)S(1)} %bitcast.234, bf16[8,1440,576]{1,0,2:T(8,128)(2,1)} %dot_general.15), kind=kOutput, calls=%fused_computation.12 | convolution fusion | flops 3400335360 | bytes 19464192 | tf_op jit(solution)/shard_map/dot_general | solution.py:56
  120.7 33.1 %all-to-all-start = ((s32[1,8,1024]{2,0,1:T(1,128)}), s32[1,8,1024]{2,0,1:T(1,128)S(1)}, u32[]{:S(2)}, u32[]{:S(2)}) async-start(s32[1,8,1024]{2,0,1:T(1,128)} %copy.92), calls=%async_computation | async-start | bytes 65536 | tf_op jit(solution)/shard_map/all_to_all | solution.py:84
  153.9 2.1 fusion.25
  156.7 1.9 all-to-all-done
  158.6 3.4 all-to-all-start.1
  167.0 4.3 all-to-all-start.2
  171.3 89.6 %reduce-scatter.3.cloned.1.call-done = bf16[64,8,1440]{2,0,1:T(8,128)(2,1)} async-done(((bf16[256,8,1440]{2,0,1:T(8,128)(2,1)}), bf16[64,8,1440]{2,0,1:T(8,128)(2,1)}) %reduce-scatter.3.cloned.1.call-update) | async-done | bytes 1474576 | tf_op jit(solution)/shard_map/reduce_scatter | solution.py:55
  260.9 3.7 multiply_multiply_fusion.1
  264.6 5.7 copy.124
  270.2 30.6 %gather_fusion.2 = f32[8192,64]{1,0:T(8,128)} fusion(f32[64,11520]{0,1:T(8,128)} %bitcast.215, s32[8192]{0:T(1024)S(1)} %get-tuple-element.69), kind=kCustom, calls=%fused_computation.2.clone | custom fusion | bytes 4227072 | tf_op jit(solution)/shard_map/jit(_take)/gather | solution.py:92
  300.8 2.8 copy.103
  303.6 33.3 %gather_fusion.3 = f32[8192,64]{1,0:T(8,128)} fusion(f32[64,11520]{0,1:T(8,128)} %bitcast.216, s32[8192]{0:T(1024)} %get-tuple-element.68), kind=kCustom, calls=%fused_computation.3.clone | custom fusion | bytes 4227072 | tf_op jit(solution)/shard_map/jit(_take)/gather | solution.py:92
  336.9 3.8 copy.105
  340.7 33.3 %gather_fusion.1 = f32[8192,64]{1,0:T(8,128)} fusion(f32[64,11520]{0,1:T(8,128)} %bitcast.217, s32[8192]{0:T(1024)} %get-tuple-element.70), kind=kCustom, calls=%fused_computation.1.clone | custom fusion | bytes 4227072 | tf_op jit(solution)/shard_map/jit(_take)/gather | solution.py:92
  373.9 3.8 copy.101
  377.7 30.6 %gather_fusion = f32[8192,64]{1,0:T(8,128)} fusion(f32[64,11520]{0,1:T(8,128)} %bitcast.218, s32[8192]{0:T(1024)S(1)} %get-tuple-element.71), kind=kCustom, calls=%fused_computation.clone | custom fusion | bytes 4227072 | tf_op jit(solution)/shard_map/jit(_take)/gather | solution.py:92
  408.3 3.8 copy.99
  412.1 5.7 convert_bitcast_fusion
  417.8 2.9 broadcast_multiply_fusion
  420.9 2.7 copy.108
  425.4 2.8 copy.110
  429.9 2.8 copy.112
  434.5 2.8 copy.114
  437.3 47.2 %scatter_custom_fusion = f32[64,11520]{0,1:T(8,128)} fusion(s32[8192]{0:T(1024)} %bitcast.244, f32[8192,64]{1,0:T(8,128)} %copy.108, f32[]{:T(128)} %constant.32.clone.1), kind=kCustom, calls=%fused_computation.24 | custom fusion | flops 524288 | bytes 2949632 | tf_op jit(solution)/shard_map/scatter-add | solution.py:99
  484.4 45.1 %scatter_fusion = f32[64,11520]{0,1:T(8,128)} fusion(f32[64,11520]{0,1:T(8,128)} %scatter_custom_fusion, s32[8192]{0:T(1024)S(1)} %bitcast.239, f32[8192,64]{1,0:T(8,128)} %copy.110), kind=kCustom, calls=%fused_computation.5 | custom fusion | flops 524288 | bytes 6324224 | tf_op jit(solution)/shard_map/scatter-add | solution.py:99
  529.5 45.2 %scatter_fusion.1 = f32[64,11520]{0,1:T(8,128)} fusion(f32[64,11520]{0,1:T(8,128)} %scatter_fusion, s32[8192]{0:T(1024)S(1)} %bitcast.238, f32[8192,64]{1,0:T(8,128)} %copy.112), kind=kCustom, calls=%fused_computation.6 | custom fusion | flops 524288 | bytes 6324224 | tf_op jit(solution)/shard_map/scatter-add | solution.py:99
  574.7 45.1 %scatter_fusion.2 = f32[64,11520]{0,1:T(8,128)} fusion(f32[64,11520]{0,1:T(8,128)} %scatter_fusion.1, s32[8192]{0:T(1024)S(1)} %bitcast.237, f32[8192,64]{1,0:T(8,128)} %copy.114), kind=kCustom, calls=%fused_computation.7 | custom fusion | flops 524288 | bytes 6324224 | tf_op jit(solution)/shard_map/scatter-add | solution.py:99
  619.8 6.1 copy.116
  625.9 3.1 fusion.15
  630.3 3.1 collective-permute-start.3
  640.6 21.6 %copy.117 = bf16[9,64,8,1440]{3,2,1,0:T(8,128)(2,1)} copy(bf16[9,64,8,1440]{3,1,2,0:T(8,128)(2,1)S(1)} %fusion.37) | data formatting | bytes 26542080 | tf_op jit(solution)/shard_map/stack | solution.py:42
  662.3 26.8 %reshape.423 = bf16[576,11520]{1,0:T(8,128)(2,1)} reshape(bf16[9,64,8,1440]{3,2,1,0:T(8,128)(2,1)} %copy.117) | data formatting | bytes 26542080 | tf_op jit(solution)/shard_map/reshape | solution.py:43
  689.1 27.9 %dot_general.18 = bf16[8,1440,576]{1,0,2:T(8,128)(2,1)} reshape(bf16[11520,576]{0,1:T(8,128)(2,1)} %bitcast.221) | data formatting | bytes 26542080 | tf_op jit(solution)/shard_map/dot_general | solution.py:56
  717.0 24.7 %fusion.7 = bf16[256,8,1440]{2,0,1:T(8,128)(2,1)} fusion(bf16[256,576,1]{0,1,2:T(8,128)(2,1)S(1)} %bitcast.235, bf16[8,1440,576]{1,0,2:T(8,128)(2,1)} %dot_general.18), kind=kOutput, calls=%fused_computation.13 | convolution fusion | flops 3400335360 | bytes 19464192 | tf_op jit(solution)/shard_map/dot_general | solution.py:56
  742.9 49.0 %all_to_all.16 = bf16[64,8,1,1024]{3,0,2,1:T(8,128)(2,1)S(1)} all-to-all(bf16[64,8,1,1024]{3,0,2,1:T(8,128)(2,1)S(1)} %copy-done.3), channel_id=1, replica_groups=mesh['lat'=8,'chan'=4] {'lat'}, dimensions={1} | all-to-all | bytes 2097152 | tf_op jit(solution)/shard_map/all_to_all | solution.py:94
  792.2 2.5 copy.121
  794.7 88.7 %reduce-scatter.5.cloned.1.call-done = bf16[64,8,1440]{2,0,1:T(8,128)(2,1)} async-done(((bf16[256,8,1440]{2,0,1:T(8,128)(2,1)}), bf16[64,8,1440]{2,0,1:T(8,128)(2,1)}) %reduce-scatter.5.cloned.1.call-update) | async-done | bytes 1474576 | tf_op jit(solution)/shard_map/reduce_scatter | solution.py:55
  883.4 3.4 copy.120
  (83 shorter events, 34.4 us)
Async XLA Ops:
  7.2 5.0 copy-start
  7.2 7.3 copy-start.1
  7.2 253.7 %reduce-scatter.3.cloned.1.call-start = ((), (), s32[]{:S(2)}) async-start(), calls=%async_computation.6 | async-start | bytes 7864320 | tf_op jit(solution)/shard_map/reduce_scatter | solution.py:55
  7.2 8.3 collective-permute-start
  10.9 19.1 %collective-permute-start.1 = (bf16[64,8,1440]{2,1,0:T(8,128)(2,1)}, bf16[64,8,1440]{2,1,0:T(8,128)(2,1)}, u32[]{:S(2)}, u32[]{:S(2)}) collective-permute-start(bf16[64,8,1440]{2,1,0:T(8,128)(2,1)} %param.9), channel_id=1, source_target_pairs={{4,0},{8,4},{12,8},{16,12},{20,16},{24,20},{28,24},{5,1},{9,5},{13... | collective-permute-start | bytes 4423688 | tf_op jit(solution)/shard_map/ppermute | solution.py:17
  66.9 28.0 %copy-start.5 = (bf16[256,3,3,64]{0,3,2,1:T(8,128)(2,1)S(1)}, bf16[256,3,3,64]{0,3,2,1:T(8,128)(2,1)}, u32[]{:S(2)}) copy-start(bf16[256,3,3,64]{0,3,2,1:T(8,128)(2,1)} %copy.95) | copy-start | bytes 884740
  119.3 0.8 copy-start.9
  119.3 34.5 %copy-start.12 = (s32[1,8]{1,0:T(1,128)S(1)}, s32[1,8]{1,0:T(1,128)}, u32[]{:S(2)}) copy-start(s32[1,8]{1,0:T(1,128)} %param.15) | copy-start | bytes 100
  119.3 34.5 %copy-start.4 = (f32[64,1,8,1024]{3,2,1,0:T(8,128)S(1)}, f32[64,1,8,1024]{3,2,1,0:T(8,128)}, u32[]{:S(2)}) copy-start(f32[64,1,8,1024]{3,2,1,0:T(8,128)} %param.12) | copy-start | bytes 6291460
  120.1 35.9 %copy-start.6 = (bf16[4,1,8,1024]{3,2,1,0:T(8,128)(2,1)S(1)}, bf16[4,1,8,1024]{3,2,1,0:T(8,128)(2,1)}, u32[]{:S(2)}) copy-start(bf16[4,1,8,1024]{3,2,1,0:T(8,128)(2,1)} %param.13) | copy-start | bytes 196612
  120.7 37.9 %all-to-all-start = ((s32[1,8,1024]{2,0,1:T(1,128)}), s32[1,8,1024]{2,0,1:T(1,128)S(1)}, u32[]{:S(2)}, u32[]{:S(2)}) async-start(s32[1,8,1024]{2,0,1:T(1,128)} %copy.92), calls=%async_computation | async-start | bytes 65536 | tf_op jit(solution)/shard_map/all_to_all | solution.py:84
  156.0 104.8 %copy-start.10 = (f32[64]{0:T(128)S(1)}, f32[64]{0:T(128)}, u32[]{:S(2)}) copy-start(f32[64]{0:T(128)} %param.11) | copy-start | bytes 772
  158.6 8.3 all-to-all-start.1
  167.0 245.2 %all-to-all-start.2 = ((bf16[64,1,8,1024]{3,0,1,2:T(8,128)(2,1)}), bf16[64,1,8,1024]{3,0,1,2:T(8,128)(2,1)}, u32[]{:S(2)}, u32[]{:S(2)}) async-start(bf16[64,1,8,1024]{3,0,1,2:T(8,128)(2,1)} %fusion.25), calls=%async_computation.3 | async-start | bytes 2097152 | tf_op jit(solution)/shard_map/all_to_all | solution.py:77
  171.2 712.2 %reduce-scatter.5.cloned.1.call-start = ((), (), s32[]{:S(2)}) async-start(), calls=%async_computation.7 | async-start | bytes 7864320 | tf_op jit(solution)/shard_map/reduce_scatter | solution.py:55
  408.3 3.8 copy-start.7
  408.3 3.8 copy-start.8
  619.8 6.1 copy-start.2
  619.8 6.1 copy-start.11
  629.0 5.8 collective-permute-start.2
  630.3 7.9 collective-permute-start.3
  741.7 1.2 copy-start.3
Sparse Core Ops, SparseCore 0:
  119.5 141.3 reduce-scatter.2
  741.8 141.5 reduce-scatter.4
where the time goes:
time: 904 us; the launch traced here: 894 us
  local copies, waits for them, and re-layouts  333 us (37%)
  other arithmetic  217 us (24%)
  waiting for transfers between devices  181 us (20%)
  starting transfers between devices  50.1 us (6%)
  matrix products  49.2 us (5%)
  blocking collectives  49 us (5%)
  between operations  14.8 us (2%)
    scatter-add x4, other arithmetic, shards(): grad_hidden.at[:, corners[which].reshape(-1)]  183 us
    reduce_scatter x2, waiting for transfers between devices, channel_mix(): lax.psum_scatter(jnp.dot(local_weights, stacked, preferred_element_type=j...  178 us
    gather x8, local copies, waits for them, and re-layouts, shards(): jnp.take(flat_hidden, corners[which], axis=1)  142 us
    dot_general x2, local copies, waits for them, and re-layouts, channel_mix(): jnp.dot(local_weights, stacked, preferred_element_type=jnp.float32)  55.9 us
    reshape x2, local copies, waits for them, and re-layouts, tap_stack(): stacked.reshape(9 * padded_field.shape[0], row_count * padded_field.shape...  53.8 us
    dot_general x2, matrix products, channel_mix(): jnp.dot(local_weights, stacked, preferred_element_type=jnp.float32)  49.2 us
    all_to_all x1, blocking collectives, shards(): lax.all_to_all(local_departures.astype(jnp.bfloat16), 'lat', split_axis=1...  49 us
    all_to_all x1, starting transfers between devices, shards(): lax.all_to_all(cells, 'lat', split_axis=1, concat_axis=0, tiled=True)  33.1 us
  transfers between devices with their start and end apart: 9, of which 4 were waited for; matrix products, arithmetic and copies ran while one was open for 21% of the time, Pallas kernels for 0%

commit v1 on v0

--- a/solution.py
+++ b/solution.py
@@ -4,6 +4,28 @@
 from jax.sharding import PartitionSpec as P
 
 KERNEL_SPACING = 8
+
+
+def cut_along(shard, dim, devices):
+    before, after = (shard.shape[:dim], shard.shape[dim + 1 :])
+    return jnp.moveaxis(shard.reshape(*before, devices, -1, *after), dim, 0)
+
+
+def joined_along(blocks, dim):
+    blocks = jnp.moveaxis(blocks, 0, dim)
+    dims = blocks.shape
+    return blocks.reshape(*dims[:dim], dims[dim] * dims[dim + 1], *dims[dim + 2 :])
+
+
+def swapped_with_each(x, axis, split_dim, concat_dim):
+    size, index = (lax.axis_size(axis), lax.axis_index(axis))
+    blocks = cut_along(x, split_dim, size)
+    finished = [blocks[index]]
+    for step in range(1, size):
+        sent = blocks[index ^ step]
+        finished.append(lax.ppermute(sent, axis, [(i, i ^ step) for i in range(size)]))
+    blocks = jnp.stack(finished)[index ^ jnp.arange(size)]
+    return joined_along(blocks, concat_dim)
 
 
 def extended(block, sides, width):
@@ -81,7 +103,7 @@
             masked_weights.astype(jnp.bfloat16), "lat", split_axis=2, concat_axis=1, tiled=True
         ).astype(masked_weights.dtype),
     )
-    got_cells = lax.all_to_all(cells, "lat", split_axis=1, concat_axis=0, tiled=True)
+    got_cells = swapped_with_each(cells, "lat", 1, 0)
     local_cells = got_cells - lax.axis_index("lat") * row_count * width
     row_index = local_cells // width
     col_index = local_cells % width

time: 904 us -> 904 us (level)
    ppermute x0 -> x7, starting transfers between devices: none -> 37.1 us  [swapped_with_each(): lax.ppermute(sent, axis, [(i, i ^ step) for i in range(size)])]
    all_to_all x1 -> x0, starting transfers between devices: 33.1 us -> none  [shards(): lax.all_to_all(cells, 'lat', split_axis=1, concat_axis=0, tiled=True)]
    unnamed x41 -> x39, local copies, waits for them, and re-layouts: 21.5 us -> 20.2 us
  transfers between devices with their start and end apart: 9 -> 15, of which waited for: 4 -> 3; matrix products, arithmetic and copies ran while one was open for 21% -> 20% of each run, Pallas kernels for 0% -> 0%
where the time goes in v1:
time: 904 us; the launch traced here: 893 us
  local copies, waits for them, and re-layouts  332 us (37%)
  other arithmetic  216 us (24%)
  waiting for transfers between devices  178 us (20%)
  starting transfers between devices  54.6 us (6%)
  matrix products  49.2 us (5%)
  blocking collectives  49 us (5%)
  between operations  14.9 us (2%)
    scatter-add x4, other arithmetic, shards(): grad_hidden.at[:, corners[which].reshape(-1)]  182 us
    reduce_scatter x2, waiting for transfers between devices, channel_mix(): lax.psum_scatter(jnp.dot(local_weights, stacked, preferred_element_type=j...  175 us
    gather x8, local copies, waits for them, and re-layouts, shards(): jnp.take(flat_hidden, corners[which], axis=1)  141 us
    dot_general x2, local copies, waits for them, and re-layouts, channel_mix(): jnp.dot(local_weights, stacked, preferred_element_type=jnp.float32)  55.9 us
    reshape x2, local copies, waits for them, and re-layouts, tap_stack(): stacked.reshape(9 * padded_field.shape[0], row_count * padded_field.shape...  53.8 us
    dot_general x2, matrix products, channel_mix(): jnp.dot(local_weights, stacked, preferred_element_type=jnp.float32)  49.2 us
    all_to_all x1, blocking collectives, shards(): lax.all_to_all(local_departures.astype(jnp.bfloat16), 'lat', split_axis=1...  49 us
    ppermute x7, starting transfers between devices, swapped_with_each(): lax.ppermute(sent, axis, [(i, i ^ step) for i in range(size)])  37.1 us
  transfers between devices with their start and end apart: 15, of which 3 were waited for; matrix products, arithmetic and copies ran while one was open for 20% of the time, Pallas kernels for 0%

profile of v1, /device:TPU:0, one launch (start us, length us, event | category | flops | bytes accessed | tf_op | source)
XLA Modules:
  0.0 893.5 jit_solution(5450671900713569363)
XLA Ops:
  7.2 3.6 collective-permute-start.7
  15.5 3.0 fusion.65
  21.4 2.7 bitcast_dynamic-update-slice_fusion.5
  25.4 1.9 fusion.28
  30.0 2.9 fusion.61
  35.9 2.7 bitcast_dynamic-update-slice_fusion.3
  39.9 27.0 %reshape.438 = bf16[576,11520]{1,0:T(8,128)(2,1)} reshape(bf16[9,64,8,1440]{3,2,1,0:T(8,128)(2,1)} %fusion.31) | data formatting | bytes 26542080 | tf_op jit(solution)/shard_map/reshape | solution.py:65
  66.9 28.0 %dot_general.15 = bf16[8,1440,576]{1,0,2:T(8,128)(2,1)} reshape(bf16[11520,576]{0,1:T(8,128)(2,1)} %bitcast.269) | data formatting | bytes 26542080 | tf_op jit(solution)/shard_map/dot_general | solution.py:78
  94.8 24.5 %fusion.4 = bf16[256,8,1440]{2,0,1:T(8,128)(2,1)} fusion(bf16[256,576,1]{0,1,2:T(8,128)(2,1)S(1)} %bitcast.284, bf16[8,1440,576]{1,0,2:T(8,128)(2,1)} %dot_general.15), kind=kOutput, calls=%fused_computation.13 | convolution fusion | flops 3400335360 | bytes 19464192 | tf_op jit(solution)/shard_map/dot_general | solution.py:78
  120.1 4.3 collective-permute-start.6
  124.4 26.8 %collective-permute-start = (s32[1,1,1024]{2,1,0:T(1,128)S(1)}, s32[1,1,1024]{2,1,0:T(1,128)S(1)}, u32[]{:S(2)}, u32[]{:S(2)}) collective-permute-start(s32[1,1,1024]{2,1,0:T(1,128)S(1)} %get-tuple-element.66), channel_id=1, source_target_pairs={{0,4},{4,0},{8,12},{12,8},{16,20},{20,16},{24,28},{28,24},{1,5},{5... | collective-permute-start | bytes 12296 | tf_op jit(solution)/shard_map/ppermute | solution.py:26
  151.2 2.3 collective-permute-start.1
  154.7 3.8 all-to-all-start
  158.6 2.1 fusion.25
  164.1 3.0 collective-permute-done.5
  170.4 4.2 all-to-all-start.1
  174.7 86.1 %reduce-scatter.3.cloned.1.call-done = bf16[64,8,1440]{2,0,1:T(8,128)(2,1)} async-done(((bf16[256,8,1440]{2,0,1:T(8,128)(2,1)}), bf16[64,8,1440]{2,0,1:T(8,128)(2,1)}) %reduce-scatter.3.cloned.1.call-update) | async-done | bytes 1474576 | tf_op jit(solution)/shard_map/reduce_scatter | solution.py:77
  260.9 3.7 multiply_multiply_fusion.1
  264.5 5.6 copy.121
  270.2 30.4 %gather_fusion.3 = f32[8192,64]{1,0:T(8,128)} fusion(f32[64,11520]{0,1:T(8,128)} %bitcast.264, s32[8192]{0:T(1024)S(1)} %get-tuple-element.70), kind=kCustom, calls=%fused_computation.2.clone | custom fusion | bytes 4227072 | tf_op jit(solution)/shard_map/jit(_take)/gather | solution.py:114
  300.6 2.8 copy.100
  303.5 33.1 %gather_fusion.1 = f32[8192,64]{1,0:T(8,128)} fusion(f32[64,11520]{0,1:T(8,128)} %bitcast.265, s32[8192]{0:T(1024)} %get-tuple-element.72), kind=kCustom, calls=%fused_computation.clone | custom fusion | bytes 4227072 | tf_op jit(solution)/shard_map/jit(_take)/gather | solution.py:114
  336.6 3.8 copy.96
  340.4 33.1 %gather_fusion.2 = f32[8192,64]{1,0:T(8,128)} fusion(f32[64,11520]{0,1:T(8,128)} %bitcast.266, s32[8192]{0:T(1024)} %get-tuple-element.71), kind=kCustom, calls=%fused_computation.1.clone | custom fusion | bytes 4227072 | tf_op jit(solution)/shard_map/jit(_take)/gather | solution.py:114
  373.5 3.8 copy.98
  377.3 30.4 %gather_fusion.4 = f32[8192,64]{1,0:T(8,128)} fusion(f32[64,11520]{0,1:T(8,128)} %bitcast.267, s32[8192]{0:T(1024)S(1)} %get-tuple-element.69), kind=kCustom, calls=%fused_computation.3.clone | custom fusion | bytes 4227072 | tf_op jit(solution)/shard_map/jit(_take)/gather | solution.py:114
  407.8 3.8 copy.102
  411.6 5.7 convert_bitcast_fusion
  417.3 2.9 broadcast_multiply_fusion
  420.4 2.7 copy.105
  424.9 2.8 copy.107
  429.4 2.8 copy.109
  433.9 2.8 copy.111
  436.7 47.2 %scatter_custom_fusion = f32[64,11520]{0,1:T(8,128)} fusion(s32[8192]{0:T(1024)} %bitcast.290, f32[8192,64]{1,0:T(8,128)} %copy.105, f32[]{:T(128)} %constant.40.clone.1), kind=kCustom, calls=%fused_computation.25 | custom fusion | flops 524288 | bytes 2949632 | tf_op jit(solution)/shard_map/scatter-add | solution.py:121
  483.9 45.1 %scatter_fusion = f32[64,11520]{0,1:T(8,128)} fusion(f32[64,11520]{0,1:T(8,128)} %scatter_custom_fusion, s32[8192]{0:T(1024)S(1)} %bitcast.288, f32[8192,64]{1,0:T(8,128)} %copy.107), kind=kCustom, calls=%fused_computation.6 | custom fusion | flops 524288 | bytes 6324224 | tf_op jit(solution)/shard_map/scatter-add | solution.py:121
  528.9 45.2 %scatter_fusion.1 = f32[64,11520]{0,1:T(8,128)} fusion(f32[64,11520]{0,1:T(8,128)} %scatter_fusion, s32[8192]{0:T(1024)S(1)} %bitcast.287, f32[8192,64]{1,0:T(8,128)} %copy.109), kind=kCustom, calls=%fused_computation.7 | custom fusion | flops 524288 | bytes 6324224 | tf_op jit(solution)/shard_map/scatter-add | solution.py:121
  574.1 45.1 %scatter_fusion.2 = f32[64,11520]{0,1:T(8,128)} fusion(f32[64,11520]{0,1:T(8,128)} %scatter_fusion.1, s32[8192]{0:T(1024)S(1)} %bitcast.286, f32[8192,64]{1,0:T(8,128)} %copy.111), kind=kCustom, calls=%fused_computation.8 | custom fusion | flops 524288 | bytes 6324224 | tf_op jit(solution)/shard_map/scatter-add | solution.py:121
  619.2 6.2 copy.113
  625.3 3.1 fusion.15
  629.7 3.1 collective-permute-start.10
  640.0 21.6 %copy.114 = bf16[9,64,8,1440]{3,2,1,0:T(8,128)(2,1)} copy(bf16[9,64,8,1440]{3,1,2,0:T(8,128)(2,1)S(1)} %fusion.37) | data formatting | bytes 26542080 | tf_op jit(solution)/shard_map/stack | solution.py:64
  661.7 26.8 %reshape.445 = bf16[576,11520]{1,0:T(8,128)(2,1)} reshape(bf16[9,64,8,1440]{3,2,1,0:T(8,128)(2,1)} %copy.114) | data formatting | bytes 26542080 | tf_op jit(solution)/shard_map/reshape | solution.py:65
  688.4 27.9 %dot_general.18 = bf16[8,1440,576]{1,0,2:T(8,128)(2,1)} reshape(bf16[11520,576]{0,1:T(8,128)(2,1)} %bitcast.270) | data formatting | bytes 26542080 | tf_op jit(solution)/shard_map/dot_general | solution.py:78
  716.4 24.7 %fusion.7 = bf16[256,8,1440]{2,0,1:T(8,128)(2,1)} fusion(bf16[256,576,1]{0,1,2:T(8,128)(2,1)S(1)} %bitcast.285, bf16[8,1440,576]{1,0,2:T(8,128)(2,1)} %dot_general.18), kind=kOutput, calls=%fused_computation.14 | convolution fusion | flops 3400335360 | bytes 19464192 | tf_op jit(solution)/shard_map/dot_general | solution.py:78
  742.3 49.0 %all_to_all.12 = bf16[64,8,1,1024]{3,0,2,1:T(8,128)(2,1)S(1)} all-to-all(bf16[64,8,1,1024]{3,0,2,1:T(8,128)(2,1)S(1)} %copy-done.3), channel_id=1, replica_groups=mesh['lat'=8,'chan'=4] {'lat'}, dimensions={1} | all-to-all | bytes 2097152 | tf_op jit(solution)/shard_map/all_to_all | solution.py:116
  791.6 2.5 copy.118
  794.2 88.7 %reduce-scatter.5.cloned.1.call-done = bf16[64,8,1440]{2,0,1:T(8,128)(2,1)} async-done(((bf16[256,8,1440]{2,0,1:T(8,128)(2,1)}), bf16[64,8,1440]{2,0,1:T(8,128)(2,1)}) %reduce-scatter.5.cloned.1.call-update) | async-done | bytes 1474576 | tf_op jit(solution)/shard_map/reduce_scatter | solution.py:77
  882.9 3.4 copy.117
  (98 shorter events, 39.5 us)
Async XLA Ops:
  7.2 5.0 copy-start
  7.2 7.3 copy-start.1
  7.2 253.7 %reduce-scatter.3.cloned.1.call-start = ((), (), s32[]{:S(2)}) async-start(), calls=%async_computation.5 | async-start | bytes 7864320 | tf_op jit(solution)/shard_map/reduce_scatter | solution.py:77
  7.2 8.3 collective-permute-start.7
  10.9 19.1 %collective-permute-start.8 = (bf16[64,8,1440]{2,1,0:T(8,128)(2,1)}, bf16[64,8,1440]{2,1,0:T(8,128)(2,1)}, u32[]{:S(2)}, u32[]{:S(2)}) collective-permute-start(bf16[64,8,1440]{2,1,0:T(8,128)(2,1)} %param.9), channel_id=1, source_target_pairs={{4,0},{8,4},{12,8},{16,12},{20,16},{24,20},{28,24},{5,1},{9,5},{13... | collective-permute-start | bytes 4423688 | tf_op jit(solution)/shard_map/ppermute | solution.py:39
  66.9 28.0 %copy-start.5 = (bf16[256,3,3,64]{0,3,2,1:T(8,128)(2,1)S(1)}, bf16[256,3,3,64]{0,3,2,1:T(8,128)(2,1)}, u32[]{:S(2)}) copy-start(bf16[256,3,3,64]{0,3,2,1:T(8,128)(2,1)} %copy.92) | copy-start | bytes 884740
  119.4 0.8 copy-start.9
  119.4 34.6 %copy-start.12 = (s32[1,8]{1,0:T(1,128)S(1)}, s32[1,8]{1,0:T(1,128)}, u32[]{:S(2)}) copy-start(s32[1,8]{1,0:T(1,128)} %param.15) | copy-start | bytes 100
  119.4 34.7 %copy-start.6 = (bf16[4,1,8,1024]{3,2,1,0:T(8,128)(2,1)S(1)}, bf16[4,1,8,1024]{3,2,1,0:T(8,128)(2,1)}, u32[]{:S(2)}) copy-start(bf16[4,1,8,1024]{3,2,1,0:T(8,128)(2,1)} %param.13) | copy-start | bytes 196612
  119.4 39.2 %copy-start.4 = (f32[64,1,8,1024]{3,2,1,0:T(8,128)S(1)}, f32[64,1,8,1024]{3,2,1,0:T(8,128)}, u32[]{:S(2)}) copy-start(f32[64,1,8,1024]{3,2,1,0:T(8,128)} %param.12) | copy-start | bytes 6291460
  120.1 40.6 %collective-permute-start.6 = (s32[1,1,1024]{2,1,0:T(1,128)S(1)}, s32[1,1,1024]{2,1,0:T(1,128)S(1)}, u32[]{:S(2)}, u32[]{:S(2)}) collective-permute-start(s32[1,1,1024]{2,1,0:T(1,128)S(1)} %get-tuple-element.61), channel_id=1, source_target_pairs={{0,28},{4,24},{8,20},{12,16},{16,12},{20,8},{24,4},{28,0},{1,29},{... | collective-permute-start | bytes 12296 | tf_op jit(solution)/shard_map/ppermute | solution.py:26
  124.4 38.1 %collective-permute-start = (s32[1,1,1024]{2,1,0:T(1,128)S(1)}, s32[1,1,1024]{2,1,0:T(1,128)S(1)}, u32[]{:S(2)}, u32[]{:S(2)}) collective-permute-start(s32[1,1,1024]{2,1,0:T(1,128)S(1)} %get-tuple-element.66), channel_id=1, source_target_pairs={{0,4},{4,0},{8,12},{12,8},{16,20},{20,16},{24,28},{28,24},{1,5},{5... | collective-permute-start | bytes 12296 | tf_op jit(solution)/shard_map/ppermute | solution.py:26
  151.2 12.8 %collective-permute-start.1 = (s32[1,1,1024]{2,1,0:T(1,128)S(1)}, s32[1,1,1024]{2,1,0:T(1,128)S(1)}, u32[]{:S(2)}, u32[]{:S(2)}) collective-permute-start(s32[1,1,1024]{2,1,0:T(1,128)S(1)} %get-tuple-element.65), channel_id=1, source_target_pairs={{0,8},{4,12},{8,0},{12,4},{16,24},{20,28},{24,16},{28,20},{1,9},{5... | collective-permute-start | bytes 12296 | tf_op jit(solution)/shard_map/ppermute | solution.py:26
  153.6 10.5 %collective-permute-start.2 = (s32[1,1,1024]{2,1,0:T(1,128)S(1)}, s32[1,1,1024]{2,1,0:T(1,128)S(1)}, u32[]{:S(2)}, u32[]{:S(2)}) collective-permute-start(s32[1,1,1024]{2,1,0:T(1,128)S(1)} %get-tuple-element.64), channel_id=1, source_target_pairs={{0,12},{4,8},{8,4},{12,0},{16,28},{20,24},{24,20},{28,16},{1,13},{... | collective-permute-start | bytes 12296 | tf_op jit(solution)/shard_map/ppermute | solution.py:26
  153.6 10.5 %collective-permute-start.3 = (s32[1,1,1024]{2,1,0:T(1,128)S(1)}, s32[1,1,1024]{2,1,0:T(1,128)S(1)}, u32[]{:S(2)}, u32[]{:S(2)}) collective-permute-start(s32[1,1,1024]{2,1,0:T(1,128)S(1)} %get-tuple-element.63), channel_id=1, source_target_pairs={{0,16},{4,20},{8,24},{12,28},{16,0},{20,4},{24,8},{28,12},{1,17},{... | collective-permute-start | bytes 12296 | tf_op jit(solution)/shard_map/ppermute | solution.py:26
  154.7 15.7 %all-to-all-start = ((bf16[4,1,8,1024]{3,0,1,2:T(4,128)(2,1)}), bf16[4,1,8,1024]{3,0,1,2:T(4,128)(2,1)S(1)}, u32[]{:S(2)}, u32[]{:S(2)}) async-start(bf16[4,1,8,1024]{3,0,1,2:T(4,128)(2,1)} %multiply_convert_fusion), calls=%async_computation | async-start | bytes 131072 | tf_op jit(solution)/shard_map/all_to_all | solution.py:102
  160.7 100.2 %copy-start.10 = (f32[64]{0:T(128)S(1)}, f32[64]{0:T(128)}, u32[]{:S(2)}) copy-start(f32[64]{0:T(128)} %param.11) | copy-start | bytes 772
  160.7 3.4 collective-permute-start.4
  162.6 4.5 collective-permute-start.5
  170.4 241.2 %all-to-all-start.1 = ((bf16[64,1,8,1024]{3,0,1,2:T(8,128)(2,1)}), bf16[64,1,8,1024]{3,0,1,2:T(8,128)(2,1)}, u32[]{:S(2)}, u32[]{:S(2)}) async-start(bf16[64,1,8,1024]{3,0,1,2:T(8,128)(2,1)} %fusion.25), calls=%async_computation.2 | async-start | bytes 2097152 | tf_op jit(solution)/shard_map/all_to_all | solution.py:99
  174.6 708.2 %reduce-scatter.5.cloned.1.call-start = ((), (), s32[]{:S(2)}) async-start(), calls=%async_computation.6 | async-start | bytes 7864320 | tf_op jit(solution)/shard_map/reduce_scatter | solution.py:77
  407.8 3.8 copy-start.7
  407.8 3.8 copy-start.8
  619.2 6.2 copy-start.2
  619.2 6.2 copy-start.11
  628.4 5.8 collective-permute-start.9
  629.7 7.9 collective-permute-start.10
  741.1 1.2 copy-start.3
Sparse Core Ops, SparseCore 0:
  119.5 141.3 reduce-scatter.2
  741.2 141.5 reduce-scatter.4
